TPU v7x, 32 devices: a whole 2x2x4 slice. The times are simulated.
32 devices in a mesh: parts: 2 (over x), rows: 16 (over z, y, core).
Axes of the slice: x: 2, y: 2, z: 4, core: 2. Of those that a mesh axis runs over, the one named last changes fastest.
Arguments:
- rhs: float32 [3, 12288, 256], P(None, 'rows', 'parts'), parts along dimension 2, may hold values from -6 to 6
- diag_inv: float32 [3, 12288, 768], P(None, 'rows'), may hold values from -0.21875 to 0.21875
- tiles: float32 [2, 32, 768, 768], P(None, 'rows'), may hold values from -0.15625 to 0.15625
- dest: int32 [2, 16, 2], P(None, 'rows'), may hold values from 0 to 15, all different within a row; in each aligned block of 16 rows (0 to 15, 16 to 31, ..., all dimensions but the last counted through in order) at most 4 rows name the same one
- obs_weight: float32 [12288], P('rows'), may hold values from -0.108253175 to 0.108253175, as said below
Outputs:
- solution: float32 [3, 12288, 256], P(None, 'rows', 'parts'), parts along dimension 2
- observed: float32 [256], P('parts'), parts along dimension 0
There are 2 independent parts, one for each index of `parts`. A program takes and returns all parts, laid end to end along the dimension named above; an argument that names none is the same for every part. Nothing has to cross between parts.
Inputs may be any that keep to these rules, and one draw needn't show every extreme that they name: `dest`: in each of the two levels, the two entries of a supernode differ, and no supernode of the next level is named more than 4 times. `obs_weight`: finite weights.
All inputs are finite; a program needn't handle non-finite values.
Results may differ from a plain program's by a relative error of at most 0.00029.
Values sent between devices are 32-bit elements; how exact they have to be, the bound alone decides.
No kernel may reach another device: no remote copies, remote signals or barrier semaphores. Data moves between devices by JAX's collectives and lax.ppermute only.
A program may use at most 128 MiB of HBM per device.

v0:
```python
import jax
import jax.numpy as jnp
from jax import lax
from jax.sharding import PartitionSpec as P


def collect_updates(solved_block, tiles_level, pattern_level):
    products = jnp.einsum(
        "kab,bc->kac",
        tiles_level,
        solved_block,
        precision=lax.Precision.HIGHEST,
        preferred_element_type=jnp.float32,
    )
    block_rows = solved_block.shape[0]
    width = products.shape[2]
    count = lax.axis_size("rows")
    sliced = lax.all_to_all(products, "rows", split_axis=1, concat_axis=0, tiled=True)
    owners = jnp.arange(count, dtype=jnp.int32)
    flat_targets = pattern_level.reshape(-1)
    matches = (owners[:, None] == flat_targets[None, :]).astype(jnp.float32)
    partial_value = jnp.einsum("mq,qac->mac", matches, sliced, precision=lax.Precision.HIGHEST)
    returned = lax.all_to_all(partial_value, "rows", split_axis=0, concat_axis=0, tiled=True)
    return returned.reshape(block_rows, width)


def body(rhs, diag_inv, tiles, dest, obs_weight):
    pattern = lax.all_gather(dest, "rows", axis=1, tiled=True)
    current = rhs[0]
    solved_levels = []
    solved_block = current
    for section in range(3):
        solved_block = jnp.dot(
            diag_inv[section],
            current,
            precision=lax.Precision.HIGHEST,
            preferred_element_type=jnp.float32,
        )
        solved_levels.append(solved_block)
        if section < 2:
            current = rhs[section + 1] - collect_updates(
                solved_block, tiles[section], pattern[section]
            )
    partial_sum = jnp.dot(
        obs_weight,
        solved_block,
        precision=lax.Precision.HIGHEST,
        preferred_element_type=jnp.float32,
    )
    observed = lax.psum(partial_sum, "rows")
    return (jnp.stack(solved_levels), observed)


def solution(mesh):
    in_specs = (
        P(None, "rows", "parts"),
        P(None, "rows", None),
        P(None, "rows", None, None),
        P(None, "rows", None),
        P("rows"),
    )
    out_specs = (P(None, "rows", "parts"), P("parts"))
    return jax.shard_map(body, mesh=mesh, in_specs=in_specs, out_specs=out_specs, check_vma=False)
```

profile of v0, /device:TPU:0, one launch (start us, length us, event | category | flops | bytes accessed | tf_op | source)
XLA Modules:
  0.0 156.5 jit_solution(14306570408259959369)
XLA Ops:
  0.6 3.7 %fusion.10 = f32[768,128]{1,0:T(8,128)S(1)} fusion(f32[3,768,768]{2,1,0:T(8,128)} %param.6, f32[3,768,128]{2,1,0:T(8,128)} %param.5), kind=kOutput, calls=%fused_computation.10 | convolution fusion | flops 905969664 | bytes 3145728 | tf_op jit(solution)/shard_map/dot_general | solution.py:33
  4.3 7.4 %fusion.15 = f32[2,768,128]{1,2,0:T(8,128)S(1)} fusion(f32[2,2,768,768]{3,2,1,0:T(8,128)} %param.7, f32[768,128]{1,0:T(8,128)S(1)} %fusion.10), kind=kOutput, calls=%fused_computation.15 | convolution fusion | flops 1811939328 | bytes 5898240 | tf_op jit(solution)/shard_map/kab,bc->kac/dot_general | solution.py:8
  11.7 0.0 copy-start.3
  11.7 1.2 copy.23
  12.9 0.0 copy-start.1
  12.9 7.5 %all-to-all-start = ((f32[2,768,128]{2,0,1:T(2,128)}), f32[2,768,128]{2,0,1:T(2,128)S(1)}, u32[]{:S(2)}, u32[]{:S(2)}) async-start(f32[2,768,128]{2,0,1:T(2,128)} %copy.23), calls=%async_computation | async-start | bytes 1572864 | tf_op jit(solution)/shard_map/all_to_all | solution.py:18
  20.4 0.0 copy-done.3
  20.4 29.2 %all_gather.3 = s32[2,16,2]{2,0,1:T(2,128)S(1)} all-gather(s32[2,1,2]{2,0,1:T(2,128)S(1)} %bitcast.82), channel_id=1, replica_groups=mesh['parts'=2,'rows'=16] {'rows'}, dimensions={1}, use_global_device_ids=true | all-gather | bytes 272 | tf_op jit(solution)/shard_map/all_gather | solution.py:28
  49.7 0.1 eq.31
  49.8 0.0 all-to-all-done
  49.8 0.0 copy-start
  49.8 0.1 copy.24
  49.8 0.6 copy.25
  50.5 0.4 fusion.29
  50.8 0.1 copy.26
  51.0 16.7 %all_to_all.46 = f32[16,48,128]{2,1,0:T(8,128)S(1)} all-to-all(f32[16,48,128]{2,1,0:T(8,128)S(1)} %copy.26), channel_id=1, replica_groups=mesh['parts'=2,'rows'=16] {'rows'}, dimensions={0} | all-to-all | bytes 786432 | tf_op jit(solution)/shard_map/all_to_all | solution.py:23
  67.7 0.0 copy-done.1
  67.7 0.1 bitcast_subtract_fusion.1
  67.8 3.8 %fusion.8 = f32[128,768]{1,0:T(8,128)S(1)} fusion(f32[3,768,768]{2,1,0:T(8,128)} %param.6, f32[1,768,128]{2,1,0:T(8,128)S(1)} %bitcast_subtract_fusion.1), kind=kOutput, calls=%fused_computation.8 | convolution fusion | flops 905969664 | bytes 3145728 | tf_op jit(solution)/shard_map/dot_general | solution.py:33
  71.5 0.0 copy-done
  71.5 5.0 %fusion.18 = f32[2,768,128]{1,2,0:T(8,128)S(1)} fusion(f32[2,2,768,768]{3,2,1,0:T(8,128)S(1)} %copy-done, f32[128,768]{1,0:T(8,128)S(1)} %fusion.8), kind=kOutput, calls=%fused_computation.16 | convolution fusion | flops 1811939328 | bytes 5898240 | tf_op jit(solution)/shard_map/kab,bc->kac/dot_general | solution.py:8
  76.5 1.2 copy.28
  77.7 3.6 %all-to-all-start.2 = ((f32[2,768,128]{2,0,1:T(2,128)}), f32[2,768,128]{2,0,1:T(2,128)S(1)}, u32[]{:S(2)}, u32[]{:S(2)}) async-start(f32[2,768,128]{2,0,1:T(2,128)} %copy.28), calls=%async_computation.2 | async-start | bytes 1572864 | tf_op jit(solution)/shard_map/all_to_all | solution.py:18
  81.3 0.1 eq.35
  81.4 18.6 %all-to-all-done.2 = f32[2,768,128]{2,0,1:T(2,128)S(1)} async-done(((f32[2,768,128]{2,0,1:T(2,128)}), f32[2,768,128]{2,0,1:T(2,128)S(1)}, u32[]{:S(2)}, u32[]{:S(2)}) %all-to-all-start.2) | async-done | bytes 786464 | tf_op jit(solution)/shard_map/all_to_all | solution.py:18
  99.9 0.1 copy.29
  100.0 0.0 copy-start.2
  100.0 0.6 copy.30
  100.6 0.4 fusion.32
  101.0 0.9 copy.31
  101.9 5.3 %all-to-all-start.3 = ((f32[16,48,128]{2,1,0:T(8,128)}), f32[16,48,128]{2,1,0:T(8,128)S(1)}, u32[]{:S(2)}, u32[]{:S(2)}) async-start(f32[16,48,128]{2,1,0:T(8,128)} %copy.31), calls=%async_computation.3 | async-start | bytes 786432 | tf_op jit(solution)/shard_map/all_to_all | solution.py:23
  107.2 0.0 copy-done.2
  107.3 0.2 copy.27
  107.4 12.0 %all-to-all-done.3 = f32[16,48,128]{2,1,0:T(8,128)S(1)} async-done(((f32[16,48,128]{2,1,0:T(8,128)}), f32[16,48,128]{2,1,0:T(8,128)S(1)}, u32[]{:S(2)}, u32[]{:S(2)}) %all-to-all-start.3) | async-done | bytes 393248 | tf_op jit(solution)/shard_map/all_to_all | solution.py:23
  119.4 3.7 %fusion.6 = f32[128,768]{0,1:T(8,128)S(1)} fusion(f32[3,768,768]{2,1,0:T(8,128)} %param.6, f32[1,768,128]{2,1,0:T(8,128)S(1)} %bitcast_subtract_fusion), kind=kOutput, calls=%fused_computation.6 | convolution fusion | flops 905969664 | bytes 3145728 | tf_op jit(solution)/shard_map/dot_general | solution.py:33
  123.1 0.3 convolution_bitcast_fusion
  123.4 32.0 %psum.7 = f32[128]{0:T(128)} all-reduce(f32[128]{0:T(128)S(1)} %convolution_bitcast_fusion), channel_id=1, replica_groups=mesh['parts'=2,'rows'=16] {'rows'}, use_global_device_ids=true, to_apply=%region_0.0 | all-reduce | flops 128 | bytes 1024 | tf_op jit(solution)/shard_map/psum | solution.py:50
  155.4 1.1 pad_maximum_fusion
  (3 shorter events, 0.1 us)
Async XLA Ops:
  11.7 8.7 %copy-start.3 = (s32[2,1,2]{2,1,0:T(1,128)S(1)}, s32[2,1,2]{2,1,0:T(1,128)}, u32[]{:S(2)}) copy-start(s32[2,1,2]{2,1,0:T(1,128)} %param.8) | copy-start | bytes 52
  12.9 54.8 %copy-start.1 = (f32[3,768,128]{2,1,0:T(8,128)S(1)}, f32[3,768,128]{2,1,0:T(8,128)}, u32[]{:S(2)}) copy-start(f32[3,768,128]{2,1,0:T(8,128)} %param.5) | copy-start | bytes 3538948
  12.9 36.9 %all-to-all-start = ((f32[2,768,128]{2,0,1:T(2,128)}), f32[2,768,128]{2,0,1:T(2,128)S(1)}, u32[]{:S(2)}, u32[]{:S(2)}) async-start(f32[2,768,128]{2,0,1:T(2,128)} %copy.23), calls=%async_computation | async-start | bytes 1572864 | tf_op jit(solution)/shard_map/all_to_all | solution.py:18
  49.8 21.8 %copy-start = (f32[2,2,768,768]{3,2,1,0:T(8,128)S(1)}, f32[2,2,768,768]{3,2,1,0:T(8,128)}, u32[]{:S(2)}) copy-start(f32[2,2,768,768]{3,2,1,0:T(8,128)} %param.7) | copy-start | bytes 28311556
  77.7 22.3 %all-to-all-start.2 = ((f32[2,768,128]{2,0,1:T(2,128)}), f32[2,768,128]{2,0,1:T(2,128)S(1)}, u32[]{:S(2)}, u32[]{:S(2)}) async-start(f32[2,768,128]{2,0,1:T(2,128)} %copy.28), calls=%async_computation.2 | async-start | bytes 1572864 | tf_op jit(solution)/shard_map/all_to_all | solution.py:18
  100.0 7.2 %copy-start.2 = (f32[768]{0:T(1024)S(1)}, f32[768]{0:T(1024)}, u32[]{:S(2)}) copy-start(f32[768]{0:T(1024)} %param.9) | copy-start | bytes 9220
  101.9 17.5 %all-to-all-start.3 = ((f32[16,48,128]{2,1,0:T(8,128)}), f32[16,48,128]{2,1,0:T(8,128)S(1)}, u32[]{:S(2)}, u32[]{:S(2)}) async-start(f32[16,48,128]{2,1,0:T(8,128)} %copy.31), calls=%async_computation.3 | async-start | bytes 786432 | tf_op jit(solution)/shard_map/all_to_all | solution.py:23
where the time goes:
time: 157 us
  blocking collectives  77.9 us (50%)
  waiting for transfers between devices  30.5 us (19%)
  matrix products  24.5 us (16%)
  starting transfers between devices  16.5 us (11%)
  local copies, waits for them, and re-layouts  5.05 us (3%)
    psum x1, blocking collectives, body(): observed = lax.psum(partial_sum, 'rows')  32 us
    all_gather x1, blocking collectives, body(): pattern = lax.all_gather(dest, 'rows', axis=1, tiled=True)  29.2 us
    all_to_all x2, waiting for transfers between devices, collect_updates(): lax.all_to_all(products, 'rows', split_axis=1, concat_axis=0, tiled=True)  18.6 us
    all_to_all x1, blocking collectives, collect_updates(): lax.all_to_all(partial_value, 'rows', split_axis=0, concat_axis=0, tiled=...  16.7 us
    dot_general x2, matrix products, collect_updates(): jnp.einsum('kab,bc->kac', tiles_level, solved_block, precision=lax.Precis...  12.3 us
    all_to_all x1, waiting for transfers between devices, collect_updates(): lax.all_to_all(partial_value, 'rows', split_axis=0, concat_axis=0, tiled=...  12 us
    all_to_all x2, starting transfers between devices, collect_updates(): lax.all_to_all(products, 'rows', split_axis=1, concat_axis=0, tiled=True)  11.2 us
    dot_general x3, matrix products, body(): jnp.dot(diag_inv[section], current, precision=lax.Precision.HIGHEST, pref...  11.1 us
  transfers between devices with their start and end apart: 3, of which 2 were waited for; matrix products, arithmetic and copies ran while one was open for 0% of the time, Pallas kernels for 0%

commit v1 on v0

--- a/solution.py
+++ b/solution.py
@@ -47,7 +47,7 @@
         precision=lax.Precision.HIGHEST,
         preferred_element_type=jnp.float32,
     )
-    observed = lax.psum(partial_sum, "rows")
+    observed = jnp.sum(lax.all_gather(partial_sum, "rows"), axis=0)
     return (jnp.stack(solved_levels), observed)
 
 

time: 157 us -> 145 us (0.924)
  blocking collectives: 77.9 us -> 65 us
    psum x1 -> x0, blocking collectives: 32 us -> none  [body(): observed = lax.psum(partial_sum, 'rows')]
    all_gather x0 -> x1, blocking collectives: none -> 19.1 us  [body(): observed = jnp.sum(lax.all_gather(partial_sum, 'rows'), axis=0)]
where the time goes in v1:
time: 145 us; the launch traced here: 144 us
  blocking collectives  65 us (45%)
  waiting for transfers between devices  30.5 us (21%)
  matrix products  24.5 us (17%)
  starting transfers between devices  16.5 us (11%)
  local copies, waits for them, and re-layouts  5.05 us (3%)
  other arithmetic  1.73 us (1%)
    all_gather x1, blocking collectives, body(): pattern = lax.all_gather(dest, 'rows', axis=1, tiled=True)  29.2 us
    all_gather x1, blocking collectives, body(): observed = jnp.sum(lax.all_gather(partial_sum, 'rows'), axis=0)  19.1 us
    all_to_all x2, waiting for transfers between devices, collect_updates(): lax.all_to_all(products, 'rows', split_axis=1, concat_axis=0, tiled=True)  18.6 us
    all_to_all x1, blocking collectives, collect_updates(): lax.all_to_all(partial_value, 'rows', split_axis=0, concat_axis=0, tiled=...  16.7 us
    dot_general x2, matrix products, collect_updates(): jnp.einsum('kab,bc->kac', tiles_level, solved_block, precision=lax.Precis...  12.3 us
    all_to_all x1, waiting for transfers between devices, collect_updates(): lax.all_to_all(partial_value, 'rows', split_axis=0, concat_axis=0, tiled=...  12 us
    all_to_all x2, starting transfers between devices, collect_updates(): lax.all_to_all(products, 'rows', split_axis=1, concat_axis=0, tiled=True)  11.2 us
    dot_general x3, matrix products, body(): jnp.dot(diag_inv[section], current, precision=lax.Precision.HIGHEST, pref...  11.1 us
  transfers between devices with their start and end apart: 3, of which 2 were waited for; matrix products, arithmetic and copies ran while one was open for 0% of the time, Pallas kernels for 0%

profile of v1, /device:TPU:0, one launch (start us, length us, event | category | flops | bytes accessed | tf_op | source)
XLA Modules:
  0.0 144.2 jit_solution(5514744558656500553)
XLA Ops:
  0.6 3.7 %fusion.10 = f32[768,128]{1,0:T(8,128)S(1)} fusion(f32[3,768,768]{2,1,0:T(8,128)} %param.6, f32[3,768,128]{2,1,0:T(8,128)} %param.5), kind=kOutput, calls=%fused_computation.10 | convolution fusion | flops 905969664 | bytes 3145728 | tf_op jit(solution)/shard_map/dot_general | solution.py:33
  4.3 7.4 %fusion.15 = f32[2,768,128]{1,2,0:T(8,128)S(1)} fusion(f32[2,2,768,768]{3,2,1,0:T(8,128)} %param.7, f32[768,128]{1,0:T(8,128)S(1)} %fusion.10), kind=kOutput, calls=%fused_computation.15 | convolution fusion | flops 1811939328 | bytes 5898240 | tf_op jit(solution)/shard_map/kab,bc->kac/dot_general | solution.py:8
  11.7 0.0 copy-start.3
  11.7 1.2 copy.23
  12.9 0.0 copy-start.1
  12.9 7.5 %all-to-all-start = ((f32[2,768,128]{2,0,1:T(2,128)}), f32[2,768,128]{2,0,1:T(2,128)S(1)}, u32[]{:S(2)}, u32[]{:S(2)}) async-start(f32[2,768,128]{2,0,1:T(2,128)} %copy.23), calls=%async_computation | async-start | bytes 1572864 | tf_op jit(solution)/shard_map/all_to_all | solution.py:18
  20.4 0.0 copy-done.3
  20.4 29.2 %all_gather.9 = s32[2,16,2]{2,0,1:T(2,128)S(1)} all-gather(s32[2,1,2]{2,0,1:T(2,128)S(1)} %bitcast.84), channel_id=1, replica_groups=mesh['parts'=2,'rows'=16] {'rows'}, dimensions={1}, use_global_device_ids=true | all-gather | bytes 272 | tf_op jit(solution)/shard_map/all_gather | solution.py:28
  49.7 0.1 eq.31
  49.8 0.0 all-to-all-done
  49.8 0.0 copy-start
  49.8 0.1 copy.24
  49.8 0.6 copy.25
  50.5 0.4 fusion.29
  50.8 0.1 copy.26
  51.0 16.7 %all_to_all.46 = f32[16,48,128]{2,1,0:T(8,128)S(1)} all-to-all(f32[16,48,128]{2,1,0:T(8,128)S(1)} %copy.26), channel_id=1, replica_groups=mesh['parts'=2,'rows'=16] {'rows'}, dimensions={0} | all-to-all | bytes 786432 | tf_op jit(solution)/shard_map/all_to_all | solution.py:23
  67.7 0.0 copy-done.1
  67.7 0.1 bitcast_subtract_fusion.1
  67.8 3.8 %fusion.8 = f32[128,768]{1,0:T(8,128)S(1)} fusion(f32[3,768,768]{2,1,0:T(8,128)} %param.6, f32[1,768,128]{2,1,0:T(8,128)S(1)} %bitcast_subtract_fusion.1), kind=kOutput, calls=%fused_computation.8 | convolution fusion | flops 905969664 | bytes 3145728 | tf_op jit(solution)/shard_map/dot_general | solution.py:33
  71.5 0.0 copy-done
  71.5 5.0 %fusion.18 = f32[2,768,128]{1,2,0:T(8,128)S(1)} fusion(f32[2,2,768,768]{3,2,1,0:T(8,128)S(1)} %copy-done, f32[128,768]{1,0:T(8,128)S(1)} %fusion.8), kind=kOutput, calls=%fused_computation.16 | convolution fusion | flops 1811939328 | bytes 5898240 | tf_op jit(solution)/shard_map/kab,bc->kac/dot_general | solution.py:8
  76.5 1.2 copy.28
  77.7 3.6 %all-to-all-start.2 = ((f32[2,768,128]{2,0,1:T(2,128)}), f32[2,768,128]{2,0,1:T(2,128)S(1)}, u32[]{:S(2)}, u32[]{:S(2)}) async-start(f32[2,768,128]{2,0,1:T(2,128)} %copy.28), calls=%async_computation.2 | async-start | bytes 1572864 | tf_op jit(solution)/shard_map/all_to_all | solution.py:18
  81.3 0.1 eq.35
  81.4 18.6 %all-to-all-done.2 = f32[2,768,128]{2,0,1:T(2,128)S(1)} async-done(((f32[2,768,128]{2,0,1:T(2,128)}), f32[2,768,128]{2,0,1:T(2,128)S(1)}, u32[]{:S(2)}, u32[]{:S(2)}) %all-to-all-start.2) | async-done | bytes 786464 | tf_op jit(solution)/shard_map/all_to_all | solution.py:18
  99.9 0.1 copy.29
  100.0 0.0 copy-start.2
  100.0 0.6 copy.30
  100.6 0.4 fusion.32
  101.0 0.9 copy.31
  101.9 5.3 %all-to-all-start.3 = ((f32[16,48,128]{2,1,0:T(8,128)}), f32[16,48,128]{2,1,0:T(8,128)S(1)}, u32[]{:S(2)}, u32[]{:S(2)}) async-start(f32[16,48,128]{2,1,0:T(8,128)} %copy.31), calls=%async_computation.3 | async-start | bytes 786432 | tf_op jit(solution)/shard_map/all_to_all | solution.py:23
  107.2 0.0 copy-done.2
  107.3 0.2 copy.27
  107.4 12.0 %all-to-all-done.3 = f32[16,48,128]{2,1,0:T(8,128)S(1)} async-done(((f32[16,48,128]{2,1,0:T(8,128)}), f32[16,48,128]{2,1,0:T(8,128)S(1)}, u32[]{:S(2)}, u32[]{:S(2)}) %all-to-all-start.3) | async-done | bytes 393248 | tf_op jit(solution)/shard_map/all_to_all | solution.py:23
  119.4 3.7 %fusion.6 = f32[128,768]{0,1:T(8,128)S(1)} fusion(f32[3,768,768]{2,1,0:T(8,128)} %param.6, f32[1,768,128]{2,1,0:T(8,128)S(1)} %bitcast_subtract_fusion), kind=kOutput, calls=%fused_computation.6 | convolution fusion | flops 905969664 | bytes 3145728 | tf_op jit(solution)/shard_map/dot_general | solution.py:33
  123.1 0.3 convolution_bitcast_fusion
  123.4 19.1 %all-gather.1 = f32[16,1,128]{2,1,0:T(1,128)S(1)} all-gather(f32[1,1,128]{2,1,0:T(1,128)S(1)} %convolution_bitcast_fusion), channel_id=2, replica_groups=mesh['parts'=2,'rows'=16] {'rows'}, dimensions={0}, use_global_device_ids=true | all-gather | bytes 8704 | tf_op jit(solution)/shard_map/all_gather | solution.py:50
  142.5 0.5 reduce_sum.9
  143.1 1.1 pad_maximum_fusion
  (3 shorter events, 0.1 us)
Async XLA Ops:
  11.7 8.7 %copy-start.3 = (s32[2,1,2]{2,1,0:T(1,128)S(1)}, s32[2,1,2]{2,1,0:T(1,128)}, u32[]{:S(2)}) copy-start(s32[2,1,2]{2,1,0:T(1,128)} %param.8) | copy-start | bytes 52
  12.9 54.8 %copy-start.1 = (f32[3,768,128]{2,1,0:T(8,128)S(1)}, f32[3,768,128]{2,1,0:T(8,128)}, u32[]{:S(2)}) copy-start(f32[3,768,128]{2,1,0:T(8,128)} %param.5) | copy-start | bytes 3538948
  12.9 36.9 %all-to-all-start = ((f32[2,768,128]{2,0,1:T(2,128)}), f32[2,768,128]{2,0,1:T(2,128)S(1)}, u32[]{:S(2)}, u32[]{:S(2)}) async-start(f32[2,768,128]{2,0,1:T(2,128)} %copy.23), calls=%async_computation | async-start | bytes 1572864 | tf_op jit(solution)/shard_map/all_to_all | solution.py:18
  49.8 21.8 %copy-start = (f32[2,2,768,768]{3,2,1,0:T(8,128)S(1)}, f32[2,2,768,768]{3,2,1,0:T(8,128)}, u32[]{:S(2)}) copy-start(f32[2,2,768,768]{3,2,1,0:T(8,128)} %param.7) | copy-start | bytes 28311556
  77.7 22.3 %all-to-all-start.2 = ((f32[2,768,128]{2,0,1:T(2,128)}), f32[2,768,128]{2,0,1:T(2,128)S(1)}, u32[]{:S(2)}, u32[]{:S(2)}) async-start(f32[2,768,128]{2,0,1:T(2,128)} %copy.28), calls=%async_computation.2 | async-start | bytes 1572864 | tf_op jit(solution)/shard_map/all_to_all | solution.py:18
  100.0 7.2 %copy-start.2 = (f32[768]{0:T(1024)S(1)}, f32[768]{0:T(1024)}, u32[]{:S(2)}) copy-start(f32[768]{0:T(1024)} %param.9) | copy-start | bytes 9220
  101.9 17.5 %all-to-all-start.3 = ((f32[16,48,128]{2,1,0:T(8,128)}), f32[16,48,128]{2,1,0:T(8,128)S(1)}, u32[]{:S(2)}, u32[]{:S(2)}) async-start(f32[16,48,128]{2,1,0:T(8,128)} %copy.31), calls=%async_computation.3 | async-start | bytes 786432 | tf_op jit(solution)/shard_map/all_to_all | solution.py:23
